TPU v7x, 256 devices: a whole 4x4x8 slice. The times are simulated.
256 devices in a mesh: cuts: 16 (over z, core), rank: 16 (over x, y).
Axes of the slice: x: 4, y: 4, z: 8, core: 2. Of those that a mesh axis runs over, the one named last changes fastest.
Arguments:
- core_one: float32 [512, 320, 512], P('rank', 'cuts'), may hold values from -6 to 6
- core_two: float32 [512, 320, 512], P('rank', 'cuts'), may hold values from -0.25 to 0.25
- right_sketch: float32 [512, 128], replicated, may hold values from -0.25 to 0.25
- sketch_core: float32 [128, 320, 128], P(None, 'cuts'), may hold values from -0.03125 to 0.03125
Outputs:
- left_core: float32 [512, 320, 128], P('rank', 'cuts')
- middle_core: float32 [128, 320, 128], P('rank', 'cuts')
- carry: float32 [128, 512], replicated
All inputs are finite; a program needn't handle non-finite values.
Results may differ from a plain program's by a relative error of at most 0.00015.
Values sent between devices are 32-bit elements; how exact they have to be, the bound alone decides.
A program may use at most 64 MiB of HBM per device.

v0:
```python
import jax
import jax.numpy as jnp
from jax import lax
from jax.sharding import PartitionSpec as P

R = 512
NM = 320
L = 128


def orthonormalize(all_rows, own_rows, carry_of):
    highest = lax.Precision.HIGHEST
    local_gram = jnp.dot(
        own_rows.T, own_rows, precision=highest, preferred_element_type=jnp.float32
    )
    gram = lax.psum(local_gram, ("cuts", "rank"))
    factor = jnp.linalg.cholesky(gram)
    ortho = lax.linalg.triangular_solve(
        factor, all_rows, left_side=False, lower=True, transpose_a=True
    )
    carried = lax.psum(carry_of(ortho), ("cuts", "rank"))
    return (ortho, carried)


def on_device(core_one, core_two, right_sketch, sketch_core):
    highest = lax.Precision.HIGHEST
    local_rows, slices, width = core_one.shape
    sketch_width = right_sketch.shape[1]
    band = sketch_width // lax.axis_size("rank")
    sketched = jnp.einsum("anj,jc->anc", core_two, right_sketch, precision=highest)
    part_bridge = jnp.einsum("anc,bnc->ab", sketched, sketch_core, precision=highest)
    bridge_rows = lax.psum(part_bridge, "cuts")
    flat_one = core_one.reshape(local_rows * slices, width)
    first_rows = jnp.dot(
        flat_one,
        lax.all_gather(bridge_rows, "rank", axis=0, tiled=True),
        precision=highest,
        preferred_element_type=jnp.float32,
    )

    def first_carry_of(matrix):
        return jnp.dot(matrix.T, flat_one, precision=highest, preferred_element_type=jnp.float32)

    first_q, first_carry = orthonormalize(first_rows, first_rows, first_carry_of)
    left_core = (jnp.sqrt(jnp.float32(R * NM)) * first_q).reshape(local_rows, slices, sketch_width)
    offset = lax.axis_index("rank") * local_rows
    local_carry = lax.dynamic_slice_in_dim(first_carry, offset, local_rows, 1)
    projected = lax.psum_scatter(
        jnp.einsum("ba,ank->bnk", local_carry, core_two, precision=highest),
        "rank",
        scatter_dimension=0,
        tiled=True,
    )
    flat_two = projected.reshape(band * slices, width)
    second_rows = jnp.dot(
        flat_two, right_sketch, precision=highest, preferred_element_type=jnp.float32
    )

    def second_carry_of(matrix):
        return jnp.dot(matrix.T, flat_two, precision=highest, preferred_element_type=jnp.float32)

    second_flat, carry = orthonormalize(second_rows, second_rows, second_carry_of)
    second_q = second_flat.reshape(band, slices, sketch_width)
    middle_core = jnp.sqrt(jnp.float32(L * NM)) * second_q
    return (left_core, middle_core, carry)


def solution(mesh):
    placed = (P("rank", "cuts", None), P("rank", "cuts", None), P(), P(None, "cuts", None))
    return jax.shard_map(
        on_device,
        mesh=mesh,
        in_specs=placed,
        out_specs=(P("rank", "cuts", None), P("rank", "cuts", None), P()),
        check_vma=False,
    )
```

profile of v0, /device:TPU:2, one launch (start us, length us, event | category | flops | bytes accessed | tf_op | source)
XLA Modules:
  0.0 1233.6 jit_solution(7768651899658973247)
XLA Ops:
  7.2 1.3 copy-done
  8.5 2.1 fusion
  10.6 1.4 convolution_bitcast_fusion
  12.0 50.9 %psum.35 = f32[32,128]{1,0:T(8,128)S(1)} all-reduce(f32[32,128]{1,0:T(8,128)S(1)} %convolution_bitcast_fusion), channel_id=1, replica_groups=mesh['cuts'=16,'rank'=16] {'cuts'}, use_global_device_ids=true, to_apply=%region_0.0 | all-reduce | flops 4096 | bytes 32768 | tf_op jit(solution)/shard_map/psum | solution.py:32
  62.9 23.8 %all_gather.3 = f32[512,128]{1,0:T(8,128)S(1)} all-gather(f32[32,128]{1,0:T(8,128)S(1)} %psum.35), channel_id=1, replica_groups=mesh['cuts'=16,'rank'=16] {'rank'}, dimensions={0}, use_global_device_ids=true | all-gather | bytes 278528 | tf_op jit(solution)/shard_map/all_gather | solution.py:36
  86.7 3.2 copy.13
  89.9 1.5 reshape.29
  91.4 1.6 fusion.14
  92.9 1.1 fusion.15
  94.3 236.5 %all-reduce.5.cloned.1.call-done = f32[128,128]{0,1:T(8,128)} async-done(((f32[128,128]{0,1:T(8,128)}), f32[128,128]{0,1:T(8,128)}) %all-reduce.5.cloned.1.call-update) | async-done | bytes 65552 | tf_op jit(solution)/shard_map/psum | solution.py:16
  330.8 0.9 copy.15
  331.8 0.9 fusion.9
  332.6 11.7 cholesky.44
  345.0 0.7 fusion.2
  345.7 9.8 custom-call.8
  355.5 0.7 broadcast_multiply_fusion
  356.2 3.0 fusion.16
  359.2 251.8 %all-reduce.7.cloned.1.call-done = f32[128,512]{0,1:T(8,128)} async-done(((f32[128,512]{0,1:T(8,128)}), f32[128,512]{0,1:T(8,128)}) %all-reduce.7.cloned.1.call-update) | async-done | bytes 262160 | tf_op jit(solution)/shard_map/psum | solution.py:21
  611.0 6.8 fusion.10
  618.1 83.2 %reduce-scatter.2.cloned.1.call-done = f32[8,20,512]{2,0,1:T(8,128)} async-done(((f32[128,20,512]{2,0,1:T(8,128)}), f32[8,20,512]{2,0,1:T(8,128)}) %reduce-scatter.2.cloned.1.call-update) | async-done | bytes 327696 | tf_op jit(solution)/shard_map/reduce_scatter | solution.py:48
  701.3 1.2 copy.16
  703.0 1.1 fusion.18
  704.1 243.4 %all-reduce.9.cloned.1.call-done = f32[128,128]{0,1:T(8,128)} async-done(((f32[128,128]{0,1:T(8,128)}), f32[128,128]{0,1:T(8,128)}) %all-reduce.9.cloned.1.call-update) | async-done | bytes 65552 | tf_op jit(solution)/shard_map/psum | solution.py:16
  947.6 0.9 copy.18
  948.5 0.9 fusion.6
  949.3 11.7 cholesky.55
  961.7 0.7 fusion.3
  962.4 9.8 custom-call.9
  972.4 1.1 fusion.19
  973.6 0.8 copy.19
  975.1 250.3 %all-reduce.11.cloned.1.call-done = f32[128,512]{1,0:T(8,128)} async-done(((f32[128,512]{1,0:T(8,128)}), f32[128,512]{1,0:T(8,128)}) %all-reduce.11.cloned.1.call-update) | async-done | bytes 262160 | tf_op jit(solution)/shard_map/psum | solution.py:21
  1225.4 1.7 copy.29
  (25 shorter events, 3.4 us)
Async XLA Ops:
  7.2 1.3 copy-start
  7.2 3.4 copy-start.1
  7.2 323.6 %all-reduce.5.cloned.1.call-start = ((), (), s32[]{:S(2)}) async-start(), calls=%async_computation.1 | async-start | bytes 131072 | tf_op jit(solution)/shard_map/psum | solution.py:16
  94.1 516.9 %all-reduce.7.cloned.1.call-start = ((), (), s32[]{:S(2)}) async-start(), calls=%async_computation.2 | async-start | bytes 524288 | tf_op jit(solution)/shard_map/psum | solution.py:21
  359.2 342.1 %reduce-scatter.2.cloned.1.call-start = ((), (), s32[]{:S(2)}) async-start(), calls=%async_computation.3 | async-start | bytes 5570560 | tf_op jit(solution)/shard_map/reduce_scatter | solution.py:48
  617.8 84.7 %copy-start.2 = (f32[512,128]{1,0:T(8,128)S(1)}, f32[512,128]{1,0:T(8,128)}, u32[]{:S(2)}) copy-start(f32[512,128]{1,0:T(8,128)} %param.7) | copy-start | bytes 786436
  617.8 329.7 %all-reduce.9.cloned.1.call-start = ((), (), s32[]{:S(2)}) async-start(), calls=%async_computation.4 | async-start | bytes 131072 | tf_op jit(solution)/shard_map/psum | solution.py:16
  704.1 521.3 %all-reduce.11.cloned.1.call-start = ((), (), s32[]{:S(2)}) async-start(), calls=%async_computation.5 | async-start | bytes 524288 | tf_op jit(solution)/shard_map/psum | solution.py:21
Sparse Core Ops, SparseCore 0:
  94.2 236.5 all-reduce.4
  359.3 251.6 all-reduce.6
  617.9 83.3 reduce-scatter.1
  707.3 240.2 all-reduce.8
  973.7 251.5 all-reduce.10
where the time goes:
time: 1230 us
  waiting for transfers between devices  1070 us (87%)
  blocking collectives  74.6 us (6%)
  other arithmetic  47.4 us (4%)
  matrix products  19.5 us (2%)
  between operations  13.9 us (1%)
    psum x2, waiting for transfers between devices, orthonormalize(): carried = lax.psum(carry_of(ortho), ('cuts', 'rank'))  502 us
    psum x2, waiting for transfers between devices, orthonormalize(): gram = lax.psum(local_gram, ('cuts', 'rank'))  480 us
    reduce_scatter x1, waiting for transfers between devices, on_device(): lax.psum_scatter(jnp.einsum('ba,ank->bnk', local_carry, core_two, precisi...  83.2 us
    psum x1, blocking collectives, on_device(): bridge_rows = lax.psum(part_bridge, 'cuts')  50.9 us
    another operation x6, other arithmetic, orthonormalize(): factor = jnp.linalg.cholesky(gram)  24.8 us
  transfers between devices with their start and end apart: 5, of which 5 were waited for; matrix products, arithmetic and copies ran while one was open for 0% of the time, Pallas kernels for 0%

commit v1 on v0

--- a/solution.py
+++ b/solution.py
@@ -13,7 +13,7 @@
     local_gram = jnp.dot(
         own_rows.T, own_rows, precision=highest, preferred_element_type=jnp.float32
     )
-    gram = lax.psum(local_gram, ("cuts", "rank"))
+    gram = lax.psum(lax.psum(local_gram, "rank"), "cuts")
     factor = jnp.linalg.cholesky(gram)
     ortho = lax.linalg.triangular_solve(
         factor, all_rows, left_side=False, lower=True, transpose_a=True

time: 1230 us -> 1140 us (0.927)
  waiting for transfers between devices: 1070 us -> 973 us
    psum x2 -> x4, waiting for transfers between devices: 480 us -> 385 us  [orthonormalize(): gram = lax.psum(lax.psum(local_gram, 'rank'), 'cuts')]
  transfers between devices with their start and end apart: 5 -> 7, of which waited for: 5 -> 7; matrix products, arithmetic and copies ran while one was open for 0% -> 0% of each run, Pallas kernels for 0% -> 0%
where the time goes in v1:
time: 1140 us
  waiting for transfers between devices  973 us (85%)
  blocking collectives  74.6 us (7%)
  other arithmetic  47.4 us (4%)
  matrix products  19.5 us (2%)
  between operations  14.3 us (1%)
  local copies, waits for them, and re-layouts  12.2 us (1%)
    psum x2, waiting for transfers between devices, orthonormalize(): carried = lax.psum(carry_of(ortho), ('cuts', 'rank'))  505 us
    psum x4, waiting for transfers between devices, orthonormalize(): gram = lax.psum(lax.psum(local_gram, 'rank'), 'cuts')  385 us
    reduce_scatter x1, waiting for transfers between devices, on_device(): lax.psum_scatter(jnp.einsum('ba,ank->bnk', local_carry, core_two, precisi...  83.2 us
    psum x1, blocking collectives, on_device(): bridge_rows = lax.psum(part_bridge, 'cuts')  50.9 us
    another operation x6, other arithmetic, orthonormalize(): factor = jnp.linalg.cholesky(gram)  24.8 us
    all_gather x1, blocking collectives, on_device(): lax.all_gather(bridge_rows, 'rank', axis=0, tiled=True)  23.8 us
  transfers between devices with their start and end apart: 7, of which 7 were waited for; matrix products, arithmetic and copies ran while one was open for 0% of the time, Pallas kernels for 0%

profile of v1, /device:TPU:2, one launch (start us, length us, event | category | flops | bytes accessed | tf_op | source)
XLA Modules:
  0.0 1142.1 jit_solution(1248734827368792865)
XLA Ops:
  7.2 1.3 copy-done
  8.5 2.1 fusion
  10.6 1.4 convolution_bitcast_fusion
  12.0 50.9 %psum.49 = f32[32,128]{1,0:T(8,128)S(1)} all-reduce(f32[32,128]{1,0:T(8,128)S(1)} %convolution_bitcast_fusion), channel_id=1, replica_groups=mesh['cuts'=16,'rank'=16] {'cuts'}, use_global_device_ids=true, to_apply=%region_0.0 | all-reduce | flops 4096 | bytes 32768 | tf_op jit(solution)/shard_map/psum | solution.py:32
  62.9 23.8 %all_gather.3 = f32[512,128]{1,0:T(8,128)S(1)} all-gather(f32[32,128]{1,0:T(8,128)S(1)} %psum.49), channel_id=1, replica_groups=mesh['cuts'=16,'rank'=16] {'rank'}, dimensions={0}, use_global_device_ids=true | all-gather | bytes 278528 | tf_op jit(solution)/shard_map/all_gather | solution.py:36
  86.7 3.2 copy.13
  89.9 1.5 reshape.29
  91.4 1.6 fusion.14
  92.9 1.1 fusion.15
  94.1 87.9 %all-reduce.7.cloned.1.call-done = f32[128,128]{0,1:T(8,128)} async-done(((f32[128,128]{0,1:T(8,128)}), f32[128,128]{0,1:T(8,128)}) %all-reduce.7.cloned.1.call-update) | async-done | bytes 65552 | tf_op jit(solution)/shard_map/psum | solution.py:16
  182.2 102.4 %all-reduce.9.cloned.1.call-done = f32[128,128]{0,1:T(8,128)} async-done(((f32[128,128]{0,1:T(8,128)}), f32[128,128]{0,1:T(8,128)}) %all-reduce.9.cloned.1.call-update) | async-done | bytes 65552 | tf_op jit(solution)/shard_map/psum | solution.py:16
  284.7 0.9 copy.15
  285.6 0.9 fusion.9
  286.5 11.7 %cholesky.44 = f32[128,128]{1,0:T(8,128)S(1)} custom-call(f32[128,128]{1,0:T(8,128)S(1)} %fusion.9), custom_call_target="Cholesky" | custom-call | tf_op jit(solution)/shard_map/jit(cholesky)/cholesky | solution.py:17
  299.5 9.8 custom-call.8
  309.3 0.7 broadcast_multiply_fusion
  310.0 3.0 fusion.16
  313.1 253.2 %all-reduce.11.cloned.1.call-done = f32[128,512]{0,1:T(8,128)} async-done(((f32[128,512]{0,1:T(8,128)}), f32[128,512]{0,1:T(8,128)}) %all-reduce.11.cloned.1.call-update) | async-done | bytes 262160 | tf_op jit(solution)/shard_map/psum | solution.py:21
  566.3 6.8 fusion.10
  573.4 83.2 %reduce-scatter.2.cloned.1.call-done = f32[8,20,512]{2,0,1:T(8,128)} async-done(((f32[128,20,512]{2,0,1:T(8,128)}), f32[8,20,512]{2,0,1:T(8,128)}) %reduce-scatter.2.cloned.1.call-update) | async-done | bytes 327696 | tf_op jit(solution)/shard_map/reduce_scatter | solution.py:48
  656.6 1.2 copy.16
  658.2 1.1 fusion.18
  659.4 92.4 %all-reduce.13.cloned.1.call-done = f32[128,128]{0,1:T(8,128)} async-done(((f32[128,128]{0,1:T(8,128)}), f32[128,128]{0,1:T(8,128)}) %all-reduce.13.cloned.1.call-update) | async-done | bytes 65552 | tf_op jit(solution)/shard_map/psum | solution.py:16
  751.8 102.5 %all-reduce.15.cloned.1.call-done = f32[128,128]{0,1:T(8,128)} async-done(((f32[128,128]{0,1:T(8,128)}), f32[128,128]{0,1:T(8,128)}) %all-reduce.15.cloned.1.call-update) | async-done | bytes 65552 | tf_op jit(solution)/shard_map/psum | solution.py:16
  854.3 0.9 copy.18
  855.2 0.9 fusion.6
  856.1 11.7 %cholesky.55 = f32[128,128]{1,0:T(8,128)S(1)} custom-call(f32[128,128]{1,0:T(8,128)S(1)} %fusion.6), custom_call_target="Cholesky" | custom-call | tf_op jit(solution)/shard_map/jit(cholesky)/cholesky | solution.py:17
  869.1 9.8 custom-call.9
  879.2 1.1 fusion.19
  880.4 0.8 copy.19
  881.8 251.8 %all-reduce.17.cloned.1.call-done = f32[128,512]{1,0:T(8,128)} async-done(((f32[128,512]{1,0:T(8,128)}), f32[128,512]{1,0:T(8,128)}) %all-reduce.17.cloned.1.call-update) | async-done | bytes 262160 | tf_op jit(solution)/shard_map/psum | solution.py:21
  1133.6 1.7 copy.31
  (31 shorter events, 4.9 us)
Async XLA Ops:
  7.2 1.3 copy-start
  7.2 3.4 copy-start.1
  7.2 174.8 %all-reduce.7.cloned.1.call-start = ((), (), s32[]{:S(2)}) async-start(), calls=%async_computation.1 | async-start | bytes 131072 | tf_op jit(solution)/shard_map/psum | solution.py:16
  94.1 190.6 %all-reduce.9.cloned.1.call-start = ((), (), s32[]{:S(2)}) async-start(), calls=%async_computation.2 | async-start | bytes 131072 | tf_op jit(solution)/shard_map/psum | solution.py:16
  182.0 384.3 %all-reduce.11.cloned.1.call-start = ((), (), s32[]{:S(2)}) async-start(), calls=%async_computation.3 | async-start | bytes 524288 | tf_op jit(solution)/shard_map/psum | solution.py:21
  313.0 343.6 %reduce-scatter.2.cloned.1.call-start = ((), (), s32[]{:S(2)}) async-start(), calls=%async_computation.4 | async-start | bytes 5570560 | tf_op jit(solution)/shard_map/reduce_scatter | solution.py:48
  573.1 84.7 %copy-start.2 = (f32[512,128]{1,0:T(8,128)S(1)}, f32[512,128]{1,0:T(8,128)}, u32[]{:S(2)}) copy-start(f32[512,128]{1,0:T(8,128)} %param.7) | copy-start | bytes 786436
  573.1 178.6 %all-reduce.13.cloned.1.call-start = ((), (), s32[]{:S(2)}) async-start(), calls=%async_computation.5 | async-start | bytes 131072 | tf_op jit(solution)/shard_map/psum | solution.py:16
  659.3 194.9 %all-reduce.15.cloned.1.call-start = ((), (), s32[]{:S(2)}) async-start(), calls=%async_computation.6 | async-start | bytes 131072 | tf_op jit(solution)/shard_map/psum | solution.py:16
  751.8 381.9 %all-reduce.17.cloned.1.call-start = ((), (), s32[]{:S(2)}) async-start(), calls=%async_computation.7 | async-start | bytes 524288 | tf_op jit(solution)/shard_map/psum | solution.py:21
Sparse Core Ops, SparseCore 0:
  94.2 87.7 all-reduce.6
  184.3 100.3 all-reduce.8
  313.1 253.0 all-reduce.10
  573.2 83.3 reduce-scatter.1
  660.2 91.4 all-reduce.12
  753.9 100.3 all-reduce.14
  880.5 253.1 all-reduce.16

commit v2 on v0

--- a/solution.py
+++ b/solution.py
@@ -18,7 +18,7 @@
     ortho = lax.linalg.triangular_solve(
         factor, all_rows, left_side=False, lower=True, transpose_a=True
     )
-    carried = lax.psum(carry_of(ortho), ("cuts", "rank"))
+    carried = lax.psum(lax.psum(carry_of(ortho), "cuts"), "rank")
     return (ortho, carried)
 
 

time: 1230 us -> 1140 us (0.927)
  waiting for transfers between devices: 1070 us -> 974 us
    psum x2 -> x4, waiting for transfers between devices: 502 us -> 410 us  [orthonormalize(): carried = lax.psum(lax.psum(carry_of(ortho), 'cuts'), 'rank')]
  transfers between devices with their start and end apart: 5 -> 7, of which waited for: 5 -> 7; matrix products, arithmetic and copies ran while one was open for 0% -> 0% of each run, Pallas kernels for 0% -> 0%
where the time goes in v2:
time: 1140 us
  waiting for transfers between devices  974 us (85%)
  blocking collectives  74.6 us (7%)
  other arithmetic  47.4 us (4%)
  matrix products  19.5 us (2%)
  between operations  14.3 us (1%)
  local copies, waits for them, and re-layouts  12.2 us (1%)
    psum x2, waiting for transfers between devices, orthonormalize(): gram = lax.psum(local_gram, ('cuts', 'rank'))  480 us
    psum x4, waiting for transfers between devices, orthonormalize(): carried = lax.psum(lax.psum(carry_of(ortho), 'cuts'), 'rank')  410 us
    reduce_scatter x1, waiting for transfers between devices, on_device(): lax.psum_scatter(jnp.einsum('ba,ank->bnk', local_carry, core_two, precisi...  84.1 us
    psum x1, blocking collectives, on_device(): bridge_rows = lax.psum(part_bridge, 'cuts')  50.9 us
    another operation x6, other arithmetic, orthonormalize(): factor = jnp.linalg.cholesky(gram)  24.8 us
    all_gather x1, blocking collectives, on_device(): lax.all_gather(bridge_rows, 'rank', axis=0, tiled=True)  23.8 us
  transfers between devices with their start and end apart: 7, of which 7 were waited for; matrix products, arithmetic and copies ran while one was open for 0% of the time, Pallas kernels for 0%

profile of v2, /device:TPU:2, one launch (start us, length us, event | category | flops | bytes accessed | tf_op | source)
XLA Modules:
  0.0 1142.9 jit_solution(15052489077970495167)
XLA Ops:
  7.2 1.3 copy-done
  8.5 2.1 fusion
  10.6 1.4 convolution_bitcast_fusion
  12.0 50.9 %psum.49 = f32[32,128]{1,0:T(8,128)S(1)} all-reduce(f32[32,128]{1,0:T(8,128)S(1)} %convolution_bitcast_fusion), channel_id=1, replica_groups=mesh['cuts'=16,'rank'=16] {'cuts'}, use_global_device_ids=true, to_apply=%region_0.0 | all-reduce | flops 4096 | bytes 32768 | tf_op jit(solution)/shard_map/psum | solution.py:32
  62.9 23.8 %all_gather.3 = f32[512,128]{1,0:T(8,128)S(1)} all-gather(f32[32,128]{1,0:T(8,128)S(1)} %psum.49), channel_id=1, replica_groups=mesh['cuts'=16,'rank'=16] {'rank'}, dimensions={0}, use_global_device_ids=true | all-gather | bytes 278528 | tf_op jit(solution)/shard_map/all_gather | solution.py:36
  86.7 3.2 copy.13
  89.9 1.5 reshape.29
  91.4 1.6 fusion.14
  92.9 1.1 fusion.15
  94.3 236.5 %all-reduce.7.cloned.1.call-done = f32[128,128]{0,1:T(8,128)} async-done(((f32[128,128]{0,1:T(8,128)}), f32[128,128]{0,1:T(8,128)}) %all-reduce.7.cloned.1.call-update) | async-done | bytes 65552 | tf_op jit(solution)/shard_map/psum | solution.py:16
  330.8 0.9 copy.15
  331.8 0.9 fusion.9
  332.6 11.7 %cholesky.44 = f32[128,128]{1,0:T(8,128)S(1)} custom-call(f32[128,128]{1,0:T(8,128)S(1)} %fusion.9), custom_call_target="Cholesky" | custom-call | tf_op jit(solution)/shard_map/jit(cholesky)/cholesky | solution.py:17
  345.7 9.8 custom-call.8
  355.5 0.7 broadcast_multiply_fusion
  356.2 3.0 fusion.16
  359.2 107.4 %all-reduce.9.cloned.1.call-done = f32[128,512]{0,1:T(8,128)} async-done(((f32[128,512]{0,1:T(8,128)}), f32[128,512]{0,1:T(8,128)}) %all-reduce.9.cloned.1.call-update) | async-done | bytes 262160 | tf_op jit(solution)/shard_map/psum | solution.py:21
  466.7 98.3 %all-reduce.11.cloned.1.call-done = f32[128,512]{0,1:T(8,128)} async-done(((f32[128,512]{0,1:T(8,128)}), f32[128,512]{0,1:T(8,128)}) %all-reduce.11.cloned.1.call-update) | async-done | bytes 262160 | tf_op jit(solution)/shard_map/psum | solution.py:21
  565.0 6.8 fusion.10
  572.1 84.1 %reduce-scatter.2.cloned.1.call-done = f32[8,20,512]{2,0,1:T(8,128)} async-done(((f32[128,20,512]{2,0,1:T(8,128)}), f32[8,20,512]{2,0,1:T(8,128)}) %reduce-scatter.2.cloned.1.call-update) | async-done | bytes 327696 | tf_op jit(solution)/shard_map/reduce_scatter | solution.py:48
  656.2 1.2 copy.16
  657.8 1.1 fusion.18
  659.0 243.5 %all-reduce.13.cloned.1.call-done = f32[128,128]{0,1:T(8,128)} async-done(((f32[128,128]{0,1:T(8,128)}), f32[128,128]{0,1:T(8,128)}) %all-reduce.13.cloned.1.call-update) | async-done | bytes 65552 | tf_op jit(solution)/shard_map/psum | solution.py:16
  902.5 0.9 copy.18
  903.4 0.9 fusion.6
  904.3 11.7 %cholesky.55 = f32[128,128]{1,0:T(8,128)S(1)} custom-call(f32[128,128]{1,0:T(8,128)S(1)} %fusion.6), custom_call_target="Cholesky" | custom-call | tf_op jit(solution)/shard_map/jit(cholesky)/cholesky | solution.py:17
  917.3 9.8 custom-call.9
  927.4 1.1 fusion.19
  928.6 107.4 %all-reduce.15.cloned.1.call-done = f32[128,512]{1,0:T(8,128)} async-done(((f32[128,512]{1,0:T(8,128)}), f32[128,512]{1,0:T(8,128)}) %all-reduce.15.cloned.1.call-update) | async-done | bytes 262160 | tf_op jit(solution)/shard_map/psum | solution.py:21
  1036.0 0.8 copy.19
  1037.5 96.9 %all-reduce.17.cloned.1.call-done = f32[128,512]{1,0:T(8,128)} async-done(((f32[128,512]{1,0:T(8,128)}), f32[128,512]{1,0:T(8,128)}) %all-reduce.17.cloned.1.call-update) | async-done | bytes 262160 | tf_op jit(solution)/shard_map/psum | solution.py:21
  1134.4 1.7 copy.31
  (31 shorter events, 4.9 us)
Async XLA Ops:
  7.2 1.3 copy-start
  7.2 3.4 copy-start.1
  7.2 323.6 %all-reduce.7.cloned.1.call-start = ((), (), s32[]{:S(2)}) async-start(), calls=%async_computation.1 | async-start | bytes 131072 | tf_op jit(solution)/shard_map/psum | solution.py:16
  94.1 372.6 %all-reduce.9.cloned.1.call-start = ((), (), s32[]{:S(2)}) async-start(), calls=%async_computation.2 | async-start | bytes 524288 | tf_op jit(solution)/shard_map/psum | solution.py:21
  359.2 205.8 %all-reduce.11.cloned.1.call-start = ((), (), s32[]{:S(2)}) async-start(), calls=%async_computation.3 | async-start | bytes 524288 | tf_op jit(solution)/shard_map/psum | solution.py:21
  466.6 189.5 %reduce-scatter.2.cloned.1.call-start = ((), (), s32[]{:S(2)}) async-start(), calls=%async_computation.4 | async-start | bytes 5570560 | tf_op jit(solution)/shard_map/reduce_scatter | solution.py:48
  571.8 85.6 %copy-start.2 = (f32[512,128]{1,0:T(8,128)S(1)}, f32[512,128]{1,0:T(8,128)}, u32[]{:S(2)}) copy-start(f32[512,128]{1,0:T(8,128)} %param.7) | copy-start | bytes 786436
  571.8 330.6 %all-reduce.13.cloned.1.call-start = ((), (), s32[]{:S(2)}) async-start(), calls=%async_computation.5 | async-start | bytes 131072 | tf_op jit(solution)/shard_map/psum | solution.py:16
  658.9 377.1 %all-reduce.15.cloned.1.call-start = ((), (), s32[]{:S(2)}) async-start(), calls=%async_computation.6 | async-start | bytes 524288 | tf_op jit(solution)/shard_map/psum | solution.py:21
  928.5 205.8 %all-reduce.17.cloned.1.call-start = ((), (), s32[]{:S(2)}) async-start(), calls=%async_computation.7 | async-start | bytes 524288 | tf_op jit(solution)/shard_map/psum | solution.py:21
Sparse Core Ops, SparseCore 0:
  94.2 236.5 all-reduce.6
  359.3 107.2 all-reduce.8
  469.8 95.1 all-reduce.10
  571.9 84.1 reduce-scatter.1
  662.1 240.3 all-reduce.12
  928.6 107.2 all-reduce.14
  1039.2 95.1 all-reduce.16
